TPU v7x, 32 devices: a whole 2x2x4 slice. The times are simulated.
32 devices in a mesh: lon: 4 (over x, core), frame: 8 (over z, y).
Axes of the slice: x: 2, y: 2, z: 4, core: 2. Of those that a mesh axis runs over, the one named last changes fastest.
Arguments:
- layer_input: bfloat16 [8, 16, 512, 128], P('frame', None, 'lon'), may hold values from -6 to 6
- hidden_saved: bfloat16 [8, 16, 512, 128], P('frame', None, 'lon'), as said below
- conv_weight: bfloat16 [3, 3, 128, 128], replicated, may hold values from -0.1875 to 0.1875
- queries: bfloat16 [2048, 128], P('lon'), may hold values from -6 to 6
- corr_cotangent: bfloat16 [8, 49, 2048], P('frame', None, 'lon'), may hold values from -0.59765625 to 0.59765625
- window_rows: int32 [8, 2048], P('frame', 'lon'), may hold values from 0 to 9
- window_cols: int32 [8, 2048], P('frame', 'lon'), may hold values from -3 to 124
- owner_strip: int32 [8, 2048, 1], P('frame', 'lon'), may hold values from 0 to 3; in each aligned block of 512 rows (0 to 511, 512 to 1023, ..., all dimensions but the last counted through in order) at most 128 rows name the same one
Outputs:
- query_grad: float32 [2048, 128], P(('lon', 'frame'))
- first_weight_grad: float32 [3, 3, 128, 128], replicated
- second_weight_grad: float32 [3, 3, 128, 128], replicated
Inputs may be any that keep to these rules, and one draw needn't show every extreme that they name: `hidden_saved`: rectifier outputs: zero or positive, a third or more of them exactly zero. `owner_strip`: in each frame, at most 128 of the 512 tracks homed on one strip name the same owning strip.
All inputs are finite; a program needn't handle non-finite values.
Results may differ from a plain program's by a relative error of at most 0.0045.
Values may be sent and summed in bfloat16 or wider, within the bound.
A program may use at most 64 MiB of HBM per device.

v0:
```python
import math
import jax
import jax.numpy as jnp
from jax import lax
from jax.sharding import PartitionSpec as P

WIN = 7


def padded_2(value, sides, width):
    for axis, dim in sides:
        peers, length = (lax.axis_size(axis), value.shape[dim])
        up = [(i, (i + 1) % peers) for i in range(peers)]
        down = [(j, i) for i, j in up]
        last = lax.slice_in_dim(value, length - width, length, axis=dim)
        first = lax.slice_in_dim(value, 0, width, axis=dim)
        before = lax.ppermute(last, axis, up)
        after = lax.ppermute(first, axis, down)
        value = jnp.concatenate([before, value, after], axis=dim)
    return value


def from_behind(value, axis, steps):
    count = lax.axis_size(axis)
    pairs = [(source, (source + steps) % count) for source in range(count)]
    return lax.ppermute(value, axis, pairs)


def pad_rows(field):
    return jnp.pad(field, ((1, 1), (0, 0), (0, 0)))


def conv_cells(padded, weight, out_cols):
    row_count = padded.shape[0] - 2
    result = jnp.zeros((row_count, out_cols, weight.shape[3]), jnp.float32)
    for row_tap in range(3):
        for col_tap in range(3):
            window = padded[row_tap : row_tap + row_count, col_tap : col_tap + out_cols]
            result = result + jnp.einsum(
                "rci,io->rco", window, weight[row_tap, col_tap], preferred_element_type=jnp.float32
            )
    return result


def conv_back(padded, weight, out_cols):
    row_count = padded.shape[0] - 2
    result = jnp.zeros((row_count, out_cols, weight.shape[2]), jnp.float32)
    for row_tap in range(3):
        for col_tap in range(3):
            window = padded[
                2 - row_tap : 2 - row_tap + row_count, 2 - col_tap : 2 - col_tap + out_cols
            ]
            result = result + jnp.einsum(
                "rco,io->rci", window, weight[row_tap, col_tap], preferred_element_type=jnp.float32
            )
    return result


def weight_terms(padded, grad):
    row_count, col_count, out_channels = grad.shape
    flat_grad = grad.reshape(row_count * col_count, out_channels)
    tap_terms = []
    for row_tap in range(3):
        for col_tap in range(3):
            window = padded[row_tap : row_tap + row_count, col_tap : col_tap + col_count].reshape(
                row_count * col_count, padded.shape[2]
            )
            tap_terms.append(
                lax.dot_general(
                    window, flat_grad, (((0,), (0,)), ((), ())), preferred_element_type=jnp.float32
                )
            )
    return jnp.stack(tap_terms).reshape(3, 3, padded.shape[2], out_channels)


def per_device(
    layer_input,
    hidden_saved,
    conv_weight,
    queries,
    corr_cotangent,
    window_rows,
    window_cols,
    owner_strip,
):
    strip_count = lax.axis_size("lon")
    input_local = layer_input[0]
    hidden_local = hidden_saved[0]
    row_count, col_count, channels = hidden_local.shape
    track_count = queries.shape[0]
    capacity = track_count // 4
    slot_count = strip_count * capacity
    wide_cols = col_count + 6
    taps_total = WIN * WIN
    reach = 4
    stacked = jnp.stack([input_local, hidden_local])
    edged = padded_2(stacked, (("lon", 2),), reach)
    input_edged = pad_rows(edged[0, :, reach - 1 : reach + col_count + 1])
    hidden_edged = pad_rows(edged[1, :, reach - 1 : reach + col_count + 1])
    feature_wide = conv_cells(pad_rows(edged[1]), conv_weight, wide_cols).astype(jnp.bfloat16)
    owners = owner_strip[0, :, 0]
    strip_ids = jnp.arange(strip_count, dtype=jnp.int32)
    marks = (owners[:, None] == strip_ids[None, :]).astype(jnp.int32)
    before = jnp.cumsum(marks, axis=0) - marks
    position = jnp.sum(before * marks, axis=1)
    slot_index = owners * capacity + position
    cot_rows = jnp.pad(corr_cotangent[0].T, ((0, 0), (0, 128 - taps_total)))
    meta_home = jnp.stack([window_rows[0], window_cols[0] + 3], axis=1)
    payload = jnp.concatenate([queries, cot_rows], axis=1)
    send_payload = (
        jnp.zeros((slot_count, payload.shape[1]), jnp.bfloat16).at[slot_index].set(payload)
    )
    send_meta = jnp.zeros((slot_count, meta_home.shape[1]), jnp.int32).at[slot_index].set(meta_home)
    got_payload, got_meta = (
        lax.all_to_all(send_payload, "lon", split_axis=0, concat_axis=0, tiled=True),
        lax.all_to_all(send_meta, "lon", split_axis=0, concat_axis=0, tiled=True),
    )
    query_slots = got_payload[:, :channels]
    cot_slots = got_payload[:, channels : channels + taps_total]
    block_rows = math.gcd(slot_count, 512)
    block_count = slot_count // block_rows
    feature_flat = feature_wide.reshape(row_count * wide_cols, channels)
    offsets = jnp.arange(WIN, dtype=jnp.int32)
    row_ids = jnp.arange(row_count, dtype=jnp.int32)
    col_ids = jnp.arange(wide_cols, dtype=jnp.int32)

    def block_step(grad_acc, block_items):
        cot_block, meta_block, query_block = block_items
        cot_square = cot_block.reshape(block_rows, WIN, WIN)
        row_hot = (
            meta_block[:, 0][:, None, None] + offsets[None, :, None] == row_ids[None, None, :]
        ).astype(jnp.bfloat16)
        col_hot = (
            meta_block[:, 1][:, None, None] + offsets[None, :, None] == col_ids[None, None, :]
        ).astype(jnp.bfloat16)
        placed_cols = jnp.einsum(
            "tij,tjh->tih", cot_square, col_hot, preferred_element_type=jnp.float32
        ).astype(jnp.bfloat16)
        spread = jnp.einsum(
            "tir,tih->trh", row_hot, placed_cols, preferred_element_type=jnp.float32
        ).astype(jnp.bfloat16)
        spread = spread.reshape(block_rows, row_count * wide_cols)
        block_grads = jnp.dot(spread, feature_flat, preferred_element_type=jnp.float32)
        grad_acc = grad_acc + lax.dot_general(
            spread, query_block, (((0,), (0,)), ((), ())), preferred_element_type=jnp.float32
        )
        return (grad_acc, block_grads)

    block_items = (
        cot_slots.reshape(block_count, block_rows, taps_total),
        got_meta.reshape(block_count, block_rows, got_meta.shape[1]),
        query_slots.reshape(block_count, block_rows, channels),
    )
    grad_flat, query_blocks = lax.scan(
        block_step, jnp.zeros((row_count * wide_cols, channels), jnp.float32), block_items
    )
    slot_grads = query_blocks.reshape(slot_count, channels)
    returned = lax.all_to_all(slot_grads, "lon", split_axis=0, concat_axis=0, tiled=True)
    home_grads = returned[slot_index]
    query_grad = lax.psum_scatter(home_grads, "frame", scatter_dimension=0, tiled=True)
    grad_wide = grad_flat.reshape(row_count, wide_cols, channels)
    from_prior = from_behind(grad_wide[:, col_count + 3 :], "lon", 1)
    from_next = from_behind(grad_wide[:, :3], "lon", -1)
    own_grad = grad_wide[:, 3 : col_count + 3]
    own_grad = own_grad.at[:, :3].add(from_prior)
    own_grad = own_grad.at[:, col_count - 3 :].add(from_next)
    grad_edged = padded_2(own_grad.astype(jnp.bfloat16), (("lon", 1),), 1)
    feature_grad = grad_edged[:, 1 : col_count + 1]
    hidden_grad = conv_back(pad_rows(grad_edged), conv_weight, col_count)
    pre_grad = jnp.where(hidden_local > 0, hidden_grad, jnp.zeros_like(hidden_grad)).astype(
        jnp.bfloat16
    )
    second_term = weight_terms(hidden_edged, feature_grad)
    first_term = weight_terms(input_edged, pre_grad)
    first_sum, second_sum = lax.psum((first_term, second_term), ("lon", "frame"))
    norm_factor = 1.0 / math.sqrt(row_count * col_count * strip_count * lax.axis_size("frame"))
    return (query_grad, first_sum * norm_factor, second_sum * norm_factor)


def solution(mesh):
    placed = (
        P("frame", None, "lon", None),
        P("frame", None, "lon", None),
        P(),
        P("lon", None),
        P("frame", None, "lon"),
        P("frame", "lon"),
        P("frame", "lon"),
        P("frame", "lon", None),
    )
    return jax.shard_map(
        per_device,
        mesh=mesh,
        in_specs=placed,
        out_specs=(P(("lon", "frame"), None), P(), P()),
        check_vma=False,
    )
```

profile of v0, /device:TPU:0, one launch (start us, length us, event | category | flops | bytes accessed | tf_op | source)
XLA Modules:
  0.0 221.2 jit_solution(16327299058159711779)
XLA Ops:
  8.8 1.2 reduce-window.6
  13.4 1.8 scatter_custom_fusion
  15.9 4.2 %all-to-all-start = ((s32[4,128,2]{1,2,0:T(2,128)}), s32[4,128,2]{1,2,0:T(2,128)S(1)}, u32[]{:S(2)}, u32[]{:S(2)}) async-start(s32[4,128,2]{1,2,0:T(2,128)} %copy.76), calls=%async_computation | async-start | bytes 8192 | tf_op jit(solution)/shard_map/all_to_all | solution.py:116
  20.3 1.8 collective-permute-start.1
  22.4 3.0 %scatter_custom_fusion.1 = bf16[512,256]{1,0:T(8,128)(2,1)} fusion(s32[512]{0:T(512)S(1)} %bitcast.248, bf16[512,256]{1,0:T(8,128)(2,1)S(1)} %copy.78, bf16[]{:T(256)} %constant.86.clone.1), kind=kCustom, calls=%fused_computation.147 | custom fusion | bytes 262146 | tf_op jit(solution)/shard_map/scatter | solution.py:111
  25.4 3.4 %all-to-all-start.1 = ((bf16[4,128,256]{2,1,0:T(8,128)(2,1)}), bf16[4,128,256]{2,1,0:T(8,128)(2,1)S(1)}, u32[]{:S(2)}, u32[]{:S(2)}) async-start(bf16[4,128,256]{2,1,0:T(8,128)(2,1)} %bitcast.13), calls=%async_computation.1 | async-start | bytes 524288 | tf_op jit(solution)/shard_map/all_to_all | solution.py:115
  29.9 0.9 copy-done.3
  34.2 1.3 fusion.9
  36.1 5.9 %fusion.1 = bf16[512,16,134]{2,1,0:T(8,128)(2,1)} fusion(bf16[512,7,7]{2,1,0:T(8,128)(2,1)S(1)} %reshape.292, s32[512,7]{1,0:T(8,128)S(1)} %get-tuple-element.69, s32[512,7]{1,0:T(8,128)S(1)} %get-tuple-element.70), kind=kOutput, calls=%fused_computation.5 | convolution fusion | flops 23109632 | bytes 2274304 | tf_op jit(solution)/shard_map/while/body/eval_jaxpr/tir,tih->trh/dot_general | solution.py:139
  42.0 7.9 %copy.81 = bf16[512,16,134]{0,1,2:T(8,128)(2,1)} copy(bf16[512,16,134]{2,1,0:T(8,128)(2,1)} %fusion.1) | data formatting | bytes 4390912 | tf_op jit(solution)/shard_map/while/body/eval_jaxpr/tir,tih->trh/dot_general | solution.py:139
  49.9 2.8 %copy.83 = bf16[512,16,134]{0,2,1:T(8,128)(2,1)S(1)} copy(bf16[512,16,134]{0,1,2:T(8,128)(2,1)} %copy.81) | data formatting | bytes 4390912 | tf_op jit(solution)/shard_map/while/body/eval_jaxpr/convert_element_type | solution.py:141
  52.7 2.1 reshape.236
  54.9 2.6 %dot_general.141 = bf16[16,134,512]{2,1,0:T(8,128)(2,1)S(1)} reshape(bf16[2144,512]{1,0:T(8,128)(2,1)} %bitcast.235) | data formatting | bytes 4390912 | tf_op jit(solution)/shard_map/while/body/eval_jaxpr/dot_general | solution.py:144
  57.5 1.6 fusion.97
  60.2 1.3 collective-permute-start.3
  61.5 1.1 collective-permute-done.2
  63.7 1.8 collective-permute-start.5
  77.5 2.5 %fusion.46 = f32[512,128,1]{1,0,2:T(8,128)} fusion(bf16[512,16,134]{0,1,2:T(8,128)(2,1)S(1)} %copy-done, bf16[16,134,128]{2,1,0:T(8,128)(2,1)} %fusion.9), kind=kOutput, calls=%fused_computation.87 | convolution fusion | flops 281018368 | bytes 3006464 | tf_op jit(solution)/shard_map/while/body/eval_jaxpr/dot_general | solution.py:143
  80.0 3.4 %all-to-all-start.2 = ((f32[4,128,128]{2,1,0:T(8,128)}), f32[4,128,128]{2,1,0:T(8,128)S(1)}, u32[]{:S(2)}, u32[]{:S(2)}) async-start(f32[4,128,128]{2,1,0:T(8,128)} %bitcast.36), calls=%async_computation.2 | async-start | bytes 524288 | tf_op jit(solution)/shard_map/all_to_all | solution.py:158
  83.5 6.6 %all-to-all-done.2 = f32[4,128,128]{2,1,0:T(8,128)S(1)} async-done(((f32[4,128,128]{2,1,0:T(8,128)}), f32[4,128,128]{2,1,0:T(8,128)S(1)}, u32[]{:S(2)}, u32[]{:S(2)}) %all-to-all-start.2) | async-done | bytes 262176 | tf_op jit(solution)/shard_map/all_to_all | solution.py:158
  90.1 1.6 gather_fusion
  91.8 119.1 %all-reduce.8.cloned.1.call-done = (f32[3,3,128,128]{3,2,1,0:T(8,128)}, f32[3,3,128,128]{3,2,1,0:T(8,128)}) async-done(((f32[3,3,128,128]{3,2,1,0:T(8,128)}, f32[3,3,128,128]{3,2,1,0:T(8,128)}), (f32[3,3,128,128]{3,2,1,0:T(8,128)}, f32[3,3,128,128]{3,2,1,0:T(8,128)})) %all-reduce.8.cloned.1.call-update) | async-done | bytes 1179664 | tf_op jit(solution)/shard_map/psum | solution.py:175
  210.9 2.0 broadcast_multiply_fusion.1
  212.9 0.9 broadcast_multiply_fusion
  (106 shorter events, 24.3 us)
Async XLA Ops:
  8.0 12.1 %copy-start.9 = (bf16[1,16,128,128]{3,2,1,0:T(8,128)(2,1)S(1)}, bf16[1,16,128,128]{3,2,1,0:T(8,128)(2,1)}, u32[]{:S(2)}) copy-start(bf16[1,16,128,128]{3,2,1,0:T(8,128)(2,1)} %param.12) | copy-start | bytes 1572868
  8.0 12.2 %copy-start.1 = (bf16[1,16,128,128]{3,2,1,0:T(8,128)(2,1)S(1)}, bf16[1,16,128,128]{3,2,1,0:T(8,128)(2,1)}, u32[]{:S(2)}) copy-start(bf16[1,16,128,128]{3,2,1,0:T(8,128)(2,1)} %param.13) | copy-start | bytes 1572868
  15.9 9.5 %all-to-all-start = ((s32[4,128,2]{1,2,0:T(2,128)}), s32[4,128,2]{1,2,0:T(2,128)S(1)}, u32[]{:S(2)}, u32[]{:S(2)}) async-start(s32[4,128,2]{1,2,0:T(2,128)} %copy.76), calls=%async_computation | async-start | bytes 8192 | tf_op jit(solution)/shard_map/all_to_all | solution.py:116
  20.1 2.0 copy-start.10
  20.1 2.1 copy-start.11
  20.3 9.0 %collective-permute-start.1 = (bf16[2,16,4,128]{3,2,1,0:T(4,128)(2,1)S(1)}, bf16[2,16,4,128]{3,2,1,0:T(4,128)(2,1)S(1)}, u32[]{:S(2)}, u32[]{:S(2)}) collective-permute-start(bf16[2,16,4,128]{3,2,1,0:T(4,128)(2,1)S(1)} %get-tuple-element.64), channel_id=1, source_target_pairs={{8,0},{16,8},{24,16},{0,24},{9,1},{17,9},{25,17},{1,25},{10,2},{18... | collective-permute-start | bytes 98312 | tf_op jit(solution)/shard_map/ppermute | solution.py:18
  22.1 7.2 %collective-permute-start = (bf16[2,16,4,128]{3,2,1,0:T(4,128)(2,1)S(1)}, bf16[2,16,4,128]{3,2,1,0:T(4,128)(2,1)S(1)}, u32[]{:S(2)}, u32[]{:S(2)}) collective-permute-start(bf16[2,16,4,128]{3,2,1,0:T(4,128)(2,1)S(1)} %get-tuple-element.63), channel_id=1, source_target_pairs={{0,8},{8,16},{16,24},{24,0},{1,9},{9,17},{17,25},{25,1},{2,10},{10... | collective-permute-start | bytes 98312 | tf_op jit(solution)/shard_map/ppermute | solution.py:17
  25.4 10.1 %all-to-all-start.1 = ((bf16[4,128,256]{2,1,0:T(8,128)(2,1)}), bf16[4,128,256]{2,1,0:T(8,128)(2,1)S(1)}, u32[]{:S(2)}, u32[]{:S(2)}) async-start(bf16[4,128,256]{2,1,0:T(8,128)(2,1)} %bitcast.13), calls=%async_computation.1 | async-start | bytes 524288 | tf_op jit(solution)/shard_map/all_to_all | solution.py:115
  28.8 182.1 %all-reduce.8.cloned.1.call-start = ((), (), s32[]{:S(2)}) async-start(), calls=%async_computation.5 | async-start | bytes 2359296 | tf_op jit(solution)/shard_map/psum | solution.py:175
  29.8 1.0 copy-start.3
  35.5 6.5 %copy-start.5 = (bf16[4,128,256]{2,1,0:T(8,128)(2,1)}, bf16[4,128,256]{2,1,0:T(8,128)(2,1)S(1)}, u32[]{:S(2)}) copy-start(bf16[4,128,256]{2,1,0:T(8,128)(2,1)S(1)} %all-to-all-done.1) | copy-start | bytes 786436
  59.2 3.4 %collective-permute-start.2 = (f32[16,3,128]{2,1,0:T(4,128)S(1)}, f32[16,3,128]{2,1,0:T(4,128)S(1)}, u32[]{:S(2)}, u32[]{:S(2)}) collective-permute-start(f32[16,3,128]{2,1,0:T(4,128)S(1)} %get-tuple-element.62), channel_id=1, source_target_pairs={{0,8},{8,16},{16,24},{24,0},{1,9},{9,17},{17,25},{25,1},{2,10},{10... | collective-permute-start | bytes 73736 | tf_op jit(solution)/shard_map/ppermute | solution.py:26
  60.2 3.2 %copy-start.4 = (bf16[3,3,128,128]{3,2,1,0:T(8,128)(2,1)S(1)}, bf16[3,3,128,128]{3,2,1,0:T(8,128)(2,1)}, u32[]{:S(2)}) copy-start(bf16[3,3,128,128]{3,2,1,0:T(8,128)(2,1)} %param.14) | copy-start | bytes 884740
  60.2 2.9 %collective-permute-start.3 = (f32[16,3,128]{2,1,0:T(4,128)S(1)}, f32[16,3,128]{2,1,0:T(4,128)S(1)}, u32[]{:S(2)}, u32[]{:S(2)}) collective-permute-start(f32[16,3,128]{2,1,0:T(4,128)S(1)} %get-tuple-element.61), channel_id=1, source_target_pairs={{0,24},{8,0},{16,8},{24,16},{1,25},{9,1},{17,9},{25,17},{2,26},{10... | collective-permute-start | bytes 73736 | tf_op jit(solution)/shard_map/ppermute | solution.py:26
  63.7 5.4 %collective-permute-start.5 = (bf16[16,1,128]{2,1,0:T(2,128)(2,1)S(1)}, bf16[16,1,128]{2,1,0:T(2,128)(2,1)S(1)}, u32[]{:S(2)}, u32[]{:S(2)}) collective-permute-start(bf16[16,1,128]{2,1,0:T(2,128)(2,1)S(1)} %get-tuple-element.66), channel_id=1, source_target_pairs={{8,0},{16,8},{24,16},{0,24},{9,1},{17,9},{25,17},{1,25},{10,2},{18... | collective-permute-start | bytes 12296 | tf_op jit(solution)/shard_map/ppermute | solution.py:18
  65.5 3.6 %collective-permute-start.4 = (bf16[16,1,128]{2,1,0:T(2,128)(2,1)S(1)}, bf16[16,1,128]{2,1,0:T(2,128)(2,1)S(1)}, u32[]{:S(2)}, u32[]{:S(2)}) collective-permute-start(bf16[16,1,128]{2,1,0:T(2,128)(2,1)S(1)} %get-tuple-element.65), channel_id=1, source_target_pairs={{0,8},{8,16},{16,24},{24,0},{1,9},{9,17},{17,25},{25,1},{2,10},{10... | collective-permute-start | bytes 12296 | tf_op jit(solution)/shard_map/ppermute | solution.py:17
  69.1 0.8 copy-start.6
  71.5 1.0 copy-start.2
  75.6 1.8 copy-start
  76.0 0.8 copy-start.7
  80.0 10.1 %all-to-all-start.2 = ((f32[4,128,128]{2,1,0:T(8,128)}), f32[4,128,128]{2,1,0:T(8,128)S(1)}, u32[]{:S(2)}, u32[]{:S(2)}) async-start(f32[4,128,128]{2,1,0:T(8,128)} %bitcast.36), calls=%async_computation.2 | async-start | bytes 524288 | tf_op jit(solution)/shard_map/all_to_all | solution.py:158
  83.4 130.3 %reduce-scatter.2.cloned.1.call-start = ((), (), s32[]{:S(2)}) async-start(), calls=%async_computation.4 | async-start | bytes 294912 | tf_op jit(solution)/shard_map/reduce_scatter | solution.py:160
  210.9 2.0 copy-start.8
Sparse Core Ops, SparseCore 0:
  77.0 133.8 all-reduce.7
Sparse Core Ops, SparseCore 1:
  91.8 62.9 reduce-scatter.1
where the time goes:
time: 222 us; the launch traced here: 221 us
  waiting for transfers between devices  127 us (57%)
  local copies, waits for them, and re-layouts  28.2 us (13%)
  matrix products  23.8 us (11%)
  starting transfers between devices  17.2 us (8%)
  between operations  16 us (7%)
  other arithmetic  8.87 us (4%)
    psum x1, waiting for transfers between devices, per_device(): lax.psum((first_term, second_term), ('lon', 'frame'))  119 us
    dot_general x1, local copies, waits for them, and re-layouts, block_step(): jnp.einsum('tir,tih->trh', row_hot, placed_cols, preferred_element_type=j...  7.86 us
    all_to_all x1, waiting for transfers between devices, per_device(): lax.all_to_all(slot_grads, 'lon', split_axis=0, concat_axis=0, tiled=True)  6.61 us
    dot_general x18, matrix products, weight_terms(): lax.dot_general(window, flat_grad, (((0,), (0,)), ((), ())), preferred_el...  6.16 us
    dot_general x1, matrix products, block_step(): jnp.einsum('tir,tih->trh', row_hot, placed_cols, preferred_element_type=j...  5.92 us
    dot_general x9, matrix products, conv_cells(): jnp.einsum('rci,io->rco', window, weight[row_tap, col_tap], preferred_ele...  4.72 us
  transfers between devices with their start and end apart: 11, of which 4 were waited for; matrix products, arithmetic and copies ran while one was open for 9% of the time, Pallas kernels for 0%

commit v1 on v0

--- a/solution.py
+++ b/solution.py
@@ -1,3 +1,4 @@
+import functools
 import math
 import jax
 import jax.numpy as jnp
@@ -5,6 +6,15 @@
 from jax.sharding import PartitionSpec as P
 
 WIN = 7
+
+
+def enter_lanes(content, dev_axis, mesh_dim):
+    for nth in (dev_axis, mesh_dim):
+        content = lax.psum(content, nth)
+    return content
+
+
+guide_the_series_all = functools.partial(enter_lanes, dev_axis="lon", mesh_dim="frame")
 
 
 def padded_2(value, sides, width):
@@ -172,7 +182,7 @@
     )
     second_term = weight_terms(hidden_edged, feature_grad)
     first_term = weight_terms(input_edged, pre_grad)
-    first_sum, second_sum = lax.psum((first_term, second_term), ("lon", "frame"))
+    first_sum, second_sum = guide_the_series_all((first_term, second_term))
     norm_factor = 1.0 / math.sqrt(row_count * col_count * strip_count * lax.axis_size("frame"))
     return (query_grad, first_sum * norm_factor, second_sum * norm_factor)
 

time: 222 us -> 276 us (1.24)
  waiting for transfers between devices: 127 us -> 177 us
    reduce_scatter x1, waiting for transfers between devices: 0.01 us -> 62.3 us  [per_device(): lax.psum_scatter(home_grads, 'frame', scatter_dimension=0, tiled=True)]
    psum x1 -> x2, waiting for transfers between devices: 119 us -> 108 us  [enter_lanes(): content = lax.psum(content, nth)]
    dot_general x9, matrix products: 4.72 us -> 7.95 us  [conv_cells(): jnp.einsum('rci,io->rco', window, weight[row_tap, col_tap], preferred_ele...]
  transfers between devices with their start and end apart: 11 -> 12, of which waited for: 4 -> 5; matrix products, arithmetic and copies ran while one was open for 9% -> 8% of each run, Pallas kernels for 0% -> 0%
where the time goes in v1:
time: 276 us; the launch traced here: 274 us
  waiting for transfers between devices  177 us (64%)
  local copies, waits for them, and re-layouts  29.1 us (11%)
  matrix products  26.2 us (9%)
  starting transfers between devices  16.6 us (6%)
  between operations  14.3 us (5%)
  other arithmetic  10.9 us (4%)
    psum x2, waiting for transfers between devices, enter_lanes(): content = lax.psum(content, nth)  108 us
    reduce_scatter x1, waiting for transfers between devices, per_device(): lax.psum_scatter(home_grads, 'frame', scatter_dimension=0, tiled=True)  62.3 us
    dot_general x9, matrix products, conv_cells(): jnp.einsum('rci,io->rco', window, weight[row_tap, col_tap], preferred_ele...  7.95 us
    dot_general x1, local copies, waits for them, and re-layouts, block_step(): jnp.einsum('tir,tih->trh', row_hot, placed_cols, preferred_element_type=j...  7.86 us
    dot_general x18, matrix products, weight_terms(): lax.dot_general(window, flat_grad, (((0,), (0,)), ((), ())), preferred_el...  6.14 us
    all_to_all x1, waiting for transfers between devices, per_device(): lax.all_to_all(slot_grads, 'lon', split_axis=0, concat_axis=0, tiled=True)  5.91 us
    dot_general x1, matrix products, block_step(): jnp.einsum('tir,tih->trh', row_hot, placed_cols, preferred_element_type=j...  5.91 us
  transfers between devices with their start and end apart: 12, of which 5 were waited for; matrix products, arithmetic and copies ran while one was open for 8% of the time, Pallas kernels for 0%

profile of v1, /device:TPU:0, one launch (start us, length us, event | category | flops | bytes accessed | tf_op | source)
XLA Modules:
  0.0 274.2 jit_solution(12328404594848795233)
XLA Ops:
  8.0 1.2 reduce-window.6
  12.6 1.8 scatter_custom_fusion
  15.1 4.2 %all-to-all-start = ((s32[4,128,2]{1,2,0:T(2,128)}), s32[4,128,2]{1,2,0:T(2,128)S(1)}, u32[]{:S(2)}, u32[]{:S(2)}) async-start(s32[4,128,2]{1,2,0:T(2,128)} %copy.76), calls=%async_computation | async-start | bytes 8192 | tf_op jit(solution)/shard_map/all_to_all | solution.py:126
  19.5 1.8 collective-permute-start.1
  21.6 3.0 %scatter_custom_fusion.1 = bf16[512,256]{1,0:T(8,128)(2,1)} fusion(s32[512]{0:T(512)S(1)} %bitcast.248, bf16[512,256]{1,0:T(8,128)(2,1)S(1)} %copy.78, bf16[]{:T(256)} %constant.86.clone.1), kind=kCustom, calls=%fused_computation.147 | custom fusion | bytes 262146 | tf_op jit(solution)/shard_map/scatter | solution.py:121
  24.6 3.4 %all-to-all-start.1 = ((bf16[4,128,256]{2,1,0:T(8,128)(2,1)}), bf16[4,128,256]{2,1,0:T(8,128)(2,1)S(1)}, u32[]{:S(2)}, u32[]{:S(2)}) async-start(bf16[4,128,256]{2,1,0:T(8,128)(2,1)} %bitcast.13), calls=%async_computation.1 | async-start | bytes 524288 | tf_op jit(solution)/shard_map/all_to_all | solution.py:125
  32.5 2.2 convolution_add_fusion.5
  35.3 5.9 %fusion.1 = bf16[512,16,134]{2,1,0:T(8,128)(2,1)} fusion(bf16[512,7,7]{2,1,0:T(8,128)(2,1)S(1)} %reshape.292, s32[512,7]{1,0:T(8,128)S(1)} %get-tuple-element.71, s32[512,7]{1,0:T(8,128)S(1)} %get-tuple-element.72), kind=kOutput, calls=%fused_computation.5 | convolution fusion | flops 23109632 | bytes 2274304 | tf_op jit(solution)/shard_map/while/body/eval_jaxpr/tir,tih->trh/dot_general | solution.py:149
  41.2 7.9 %copy.81 = bf16[512,16,134]{0,1,2:T(8,128)(2,1)} copy(bf16[512,16,134]{2,1,0:T(8,128)(2,1)} %fusion.1) | data formatting | bytes 4390912 | tf_op jit(solution)/shard_map/while/body/eval_jaxpr/tir,tih->trh/dot_general | solution.py:149
  49.0 2.8 %copy.83 = bf16[512,16,134]{0,2,1:T(8,128)(2,1)S(1)} copy(bf16[512,16,134]{0,1,2:T(8,128)(2,1)} %copy.81) | data formatting | bytes 4390912 | tf_op jit(solution)/shard_map/while/body/eval_jaxpr/convert_element_type | solution.py:151
  51.9 2.1 reshape.236
  54.0 2.6 dot_general.141
  56.6 1.7 fusion.97
  60.0 1.5 collective-permute-start.3
  63.9 1.4 slice_add_fusion
  66.6 1.3 collective-permute-start.5
  79.9 38.5 %all-reduce.12.cloned.1.call-done = (f32[3,3,128,128]{3,2,1,0:T(8,128)}, f32[3,3,128,128]{3,2,1,0:T(8,128)}) async-done(((f32[3,3,128,128]{3,2,1,0:T(8,128)}, f32[3,3,128,128]{3,2,1,0:T(8,128)}), (f32[3,3,128,128]{3,2,1,0:T(8,128)}, f32[3,3,128,128]{3,2,1,0:T(8,128)})) %all-reduce.12.cloned.1.call-update) | async-done | bytes 1179664 | tf_op jit(solution)/shard_map/psum | solution.py:13
  120.5 1.5 fusion.46
  122.0 3.4 %all-to-all-start.2 = ((f32[4,128,128]{2,1,0:T(8,128)}), f32[4,128,128]{2,1,0:T(8,128)S(1)}, u32[]{:S(2)}, u32[]{:S(2)}) async-start(f32[4,128,128]{2,1,0:T(8,128)} %bitcast.36), calls=%async_computation.2 | async-start | bytes 524288 | tf_op jit(solution)/shard_map/all_to_all | solution.py:168
  125.5 5.9 %all-to-all-done.2 = f32[4,128,128]{2,1,0:T(8,128)S(1)} async-done(((f32[4,128,128]{2,1,0:T(8,128)}), f32[4,128,128]{2,1,0:T(8,128)S(1)}, u32[]{:S(2)}, u32[]{:S(2)}) %all-to-all-start.2) | async-done | bytes 262176 | tf_op jit(solution)/shard_map/all_to_all | solution.py:168
  131.4 1.6 gather_fusion
  133.0 69.5 %all-reduce.10.cloned.1.call-done = (f32[3,3,128,128]{3,2,1,0:T(8,128)}, f32[3,3,128,128]{3,2,1,0:T(8,128)}) async-done(((f32[3,3,128,128]{3,2,1,0:T(8,128)}, f32[3,3,128,128]{3,2,1,0:T(8,128)}), (f32[3,3,128,128]{3,2,1,0:T(8,128)}, f32[3,3,128,128]{3,2,1,0:T(8,128)})) %all-reduce.10.cloned.1.call-update) | async-done | bytes 1179664 | tf_op jit(solution)/shard_map/psum | solution.py:13
  202.5 2.0 broadcast_multiply_fusion.1
  205.3 62.3 %reduce-scatter.2.cloned.1.call-done = f32[64,128]{1,0:T(8,128)} async-done(((f32[512,128]{1,0:T(8,128)}), f32[64,128]{1,0:T(8,128)}) %reduce-scatter.2.cloned.1.call-update) | async-done | bytes 32784 | tf_op jit(solution)/shard_map/reduce_scatter | solution.py:170
  (111 shorter events, 30.4 us)
Async XLA Ops:
  7.2 12.1 %copy-start.10 = (bf16[1,16,128,128]{3,2,1,0:T(8,128)(2,1)S(1)}, bf16[1,16,128,128]{3,2,1,0:T(8,128)(2,1)}, u32[]{:S(2)}) copy-start(bf16[1,16,128,128]{3,2,1,0:T(8,128)(2,1)} %param.12) | copy-start | bytes 1572868
  7.2 12.2 %copy-start.4 = (bf16[1,16,128,128]{3,2,1,0:T(8,128)(2,1)S(1)}, bf16[1,16,128,128]{3,2,1,0:T(8,128)(2,1)}, u32[]{:S(2)}) copy-start(bf16[1,16,128,128]{3,2,1,0:T(8,128)(2,1)} %param.13) | copy-start | bytes 1572868
  15.1 9.5 %all-to-all-start = ((s32[4,128,2]{1,2,0:T(2,128)}), s32[4,128,2]{1,2,0:T(2,128)S(1)}, u32[]{:S(2)}, u32[]{:S(2)}) async-start(s32[4,128,2]{1,2,0:T(2,128)} %copy.76), calls=%async_computation | async-start | bytes 8192 | tf_op jit(solution)/shard_map/all_to_all | solution.py:126
  19.3 2.0 copy-start.11
  19.3 2.1 copy-start.12
  19.5 8.8 %collective-permute-start.1 = (bf16[2,16,4,128]{3,2,1,0:T(4,128)(2,1)S(1)}, bf16[2,16,4,128]{3,2,1,0:T(4,128)(2,1)S(1)}, u32[]{:S(2)}, u32[]{:S(2)}) collective-permute-start(bf16[2,16,4,128]{3,2,1,0:T(4,128)(2,1)S(1)} %get-tuple-element.66), channel_id=1, source_target_pairs={{8,0},{16,8},{24,16},{0,24},{9,1},{17,9},{25,17},{1,25},{10,2},{18... | collective-permute-start | bytes 98312 | tf_op jit(solution)/shard_map/ppermute | solution.py:28
  21.3 7.0 %collective-permute-start = (bf16[2,16,4,128]{3,2,1,0:T(4,128)(2,1)S(1)}, bf16[2,16,4,128]{3,2,1,0:T(4,128)(2,1)S(1)}, u32[]{:S(2)}, u32[]{:S(2)}) collective-permute-start(bf16[2,16,4,128]{3,2,1,0:T(4,128)(2,1)S(1)} %get-tuple-element.65), channel_id=1, source_target_pairs={{0,8},{8,16},{16,24},{24,0},{1,9},{9,17},{17,25},{25,1},{2,10},{10... | collective-permute-start | bytes 98312 | tf_op jit(solution)/shard_map/ppermute | solution.py:27
  24.6 10.1 %all-to-all-start.1 = ((bf16[4,128,256]{2,1,0:T(8,128)(2,1)}), bf16[4,128,256]{2,1,0:T(8,128)(2,1)S(1)}, u32[]{:S(2)}, u32[]{:S(2)}) async-start(bf16[4,128,256]{2,1,0:T(8,128)(2,1)} %bitcast.13), calls=%async_computation.1 | async-start | bytes 524288 | tf_op jit(solution)/shard_map/all_to_all | solution.py:125
  28.0 90.4 %all-reduce.12.cloned.1.call-start = ((), (), s32[]{:S(2)}) async-start(), calls=%async_computation.6 | async-start | bytes 2359296 | tf_op jit(solution)/shard_map/psum | solution.py:13
  28.8 1.3 copy-start.1
  34.6 6.5 %copy-start.6 = (bf16[4,128,256]{2,1,0:T(8,128)(2,1)}, bf16[4,128,256]{2,1,0:T(8,128)(2,1)S(1)}, u32[]{:S(2)}) copy-start(bf16[4,128,256]{2,1,0:T(8,128)(2,1)S(1)} %all-to-all-done.1) | copy-start | bytes 786436
  56.6 2.9 %copy-start.2 = (bf16[2,16,136,128]{3,2,1,0:T(8,128)(2,1)S(1)}, bf16[2,16,136,128]{3,2,1,0:T(8,128)(2,1)}, u32[]{:S(2)}) copy-start(bf16[2,16,136,128]{3,2,1,0:T(8,128)(2,1)} %copy-done.1) | copy-start | bytes 3342340
  59.0 3.3 %collective-permute-start.2 = (f32[16,3,128]{2,1,0:T(4,128)S(1)}, f32[16,3,128]{2,1,0:T(4,128)S(1)}, u32[]{:S(2)}, u32[]{:S(2)}) collective-permute-start(f32[16,3,128]{2,1,0:T(4,128)S(1)} %get-tuple-element.64), channel_id=1, source_target_pairs={{0,8},{8,16},{16,24},{24,0},{1,9},{9,17},{17,25},{25,1},{2,10},{10... | collective-permute-start | bytes 73736 | tf_op jit(solution)/shard_map/ppermute | solution.py:36
  60.0 6.3 %copy-start.5 = (bf16[3,3,128,128]{3,2,1,0:T(8,128)(2,1)S(1)}, bf16[3,3,128,128]{3,2,1,0:T(8,128)(2,1)}, u32[]{:S(2)}) copy-start(bf16[3,3,128,128]{3,2,1,0:T(8,128)(2,1)} %param.14) | copy-start | bytes 884740
  60.0 3.9 %collective-permute-start.3 = (f32[16,3,128]{2,1,0:T(4,128)}, f32[16,3,128]{2,1,0:T(4,128)}, u32[]{:S(2)}, u32[]{:S(2)}) collective-permute-start(f32[16,3,128]{2,1,0:T(4,128)} %get-tuple-element.63), channel_id=1, source_target_pairs={{0,24},{8,0},{16,8},{24,16},{1,25},{9,1},{17,9},{25,17},{2,26},{10... | collective-permute-start | bytes 73736 | tf_op jit(solution)/shard_map/ppermute | solution.py:36
  66.6 4.8 %collective-permute-start.5 = (bf16[16,1,128]{2,1,0:T(2,128)(2,1)S(1)}, bf16[16,1,128]{2,1,0:T(2,128)(2,1)S(1)}, u32[]{:S(2)}, u32[]{:S(2)}) collective-permute-start(bf16[16,1,128]{2,1,0:T(2,128)(2,1)S(1)} %get-tuple-element.68), channel_id=1, source_target_pairs={{8,0},{16,8},{24,16},{0,24},{9,1},{17,9},{25,17},{1,25},{10,2},{18... | collective-permute-start | bytes 12296 | tf_op jit(solution)/shard_map/ppermute | solution.py:28
  67.9 3.5 %collective-permute-start.4 = (bf16[16,1,128]{2,1,0:T(2,128)(2,1)S(1)}, bf16[16,1,128]{2,1,0:T(2,128)(2,1)S(1)}, u32[]{:S(2)}, u32[]{:S(2)}) collective-permute-start(bf16[16,1,128]{2,1,0:T(2,128)(2,1)S(1)} %get-tuple-element.67), channel_id=1, source_target_pairs={{0,8},{8,16},{16,24},{24,0},{1,9},{9,17},{17,25},{25,1},{2,10},{10... | collective-permute-start | bytes 12296 | tf_op jit(solution)/shard_map/ppermute | solution.py:27
  71.4 0.8 copy-start.7
  77.3 1.3 copy-start.3
  78.5 124.0 %all-reduce.10.cloned.1.call-start = ((), (), s32[]{:S(2)}) async-start(), calls=%async_computation.5 | async-start | bytes 2359296 | tf_op jit(solution)/shard_map/psum | solution.py:13
  118.9 1.6 copy-start
  122.0 9.4 %all-to-all-start.2 = ((f32[4,128,128]{2,1,0:T(8,128)}), f32[4,128,128]{2,1,0:T(8,128)S(1)}, u32[]{:S(2)}, u32[]{:S(2)}) async-start(f32[4,128,128]{2,1,0:T(8,128)} %bitcast.36), calls=%async_computation.2 | async-start | bytes 524288 | tf_op jit(solution)/shard_map/all_to_all | solution.py:168
  125.4 142.3 %reduce-scatter.2.cloned.1.call-start = ((), (), s32[]{:S(2)}) async-start(), calls=%async_computation.4 | async-start | bytes 294912 | tf_op jit(solution)/shard_map/reduce_scatter | solution.py:170
  202.5 2.0 copy-start.9
  (1 other events, 0.8 us)
Sparse Core Ops, SparseCore 0:
  78.6 39.7 all-reduce.11
  121.9 80.5 all-reduce.9
  206.4 61.2 reduce-scatter.1
